TPU v7x, 32 devices: a whole 2x2x4 slice. The times are simulated.
32 devices in a mesh: groups: 2 (over x), img: 16 (over z, y, core).
Axes of the slice: x: 2, y: 2, z: 4, core: 2. Of those that a mesh axis runs over, the one named last changes fastest.
Arguments:
- descriptors: bfloat16 [32, 256, 1024], P(('groups', 'img')), parts along dimension 0, may hold values from -6 to 6
- attributes: bfloat16 [32, 3, 1024], P(('groups', 'img')), parts along dimension 0, may hold values from -1 to 4, as said below
- counts: int32 [32], P('groups'), parts along dimension 0, may hold values from 256 to 1024
- owner_slot: int32 [32], P('groups'), parts along dimension 0, may hold values from 0 to 15, as said below
- pair_list: int32 [32, 2], P(('groups', 'img')), parts along dimension 0, may hold values from 0 to 15, as said below
Outputs:
- match_xy: float32 [32, 2, 1024], P(('groups', 'img')), parts along dimension 0
- col_lse: float32 [32, 1024], P(('groups', 'img')), parts along dimension 0
- col_xy: float32 [32, 2, 1024], P(('groups', 'img')), parts along dimension 0
There are 2 independent parts, one for each index of `groups`. A program takes and returns all parts, laid end to end along the dimension named above; each array names one. Nothing has to cross between parts.
Inputs may be any that keep to these rules, and one draw needn't show every extreme that they name: owner_slot is a permutation: every slot holds exactly one image id; slot s lies on the device of index s. The query image of row p is stored on the device that holds row p: owner_slot[pair_list[p,0]] == p; the partner differs from the query. `attributes`: scales lie in 0.5 to 4, coordinates in -1 to 1.
All inputs are finite; a program needn't handle non-finite values.
Results may differ from a plain program's by a relative error of at most 0.0003.
Values may be sent and summed in bfloat16 or wider, within the bound.
A program may use at most 64 MiB of HBM per device.

v0:
```python
import functools
import math

import jax
import jax.numpy as jnp
from jax import lax
from jax.experimental import pallas as pl
from jax.experimental.pallas import tpu as pltpu
from jax.sharding import PartitionSpec as P

MESH = pl.DeviceIdType.MESH
LANES = 128
ROWS = 256
ROUNDS = 4
MIN_WIDTH = 16
far_low = -1e30


def split_dot(left, right, contract):
    high = right.astype(jnp.bfloat16)
    low = (right - high.astype(jnp.float32)).astype(jnp.bfloat16)
    dims = (contract, ((), ()))
    return lax.dot_general(left, high, dims, preferred_element_type=jnp.float32) + lax.dot_general(
        left, low, dims, preferred_element_type=jnp.float32
    )


def with_ones(attr):
    ones = jnp.ones((1, attr.shape[1]), jnp.float32)
    rest = jnp.zeros((4, attr.shape[1]), jnp.float32)
    return jnp.concatenate([attr[0:1], ones, attr[1:3], rest], axis=0)


def kernel(
    n, rounds, desc, attr, counts, owner, pairs, match_o, lse_o, xy_o,
    own, own_t, own_attr, row_scale, own_rows, other_rows, other_scale, want_out, want_all, want_s,
    counts_s, owner_s, pairs_s, attr_in, attr_stage, attr_other,
    stage, partner, scores, row_top, stats_out, stats_in, merged_out, merged_in, direct_in,
    local_sem, want_ss, want_rs, attr_ss1, attr_rs1, attr_ss2, attr_rs2, ss1, rs1, ss2, rs2, ss3, rs3, ss4, rs4, ss5, rs5,
    *pieces,
):
    depth, keypoints = desc.shape[1:]
    chunks = keypoints // LANES
    parts = n // chunks
    blocks = keypoints // ROWS
    me = lax.axis_index("img")
    my_chunk = me // parts
    my_part = lax.rem(me, parts)
    round_chunks = chunks // rounds
    round_parts = n // round_chunks
    width = depth // round_parts
    early = chunks - round_chunks

    def peer(step):
        return lax.rem(me + step, n)

    def remote(src, dst, send, recv, to):
        return pltpu.make_async_remote_copy(
            src_ref=src, dst_ref=dst, send_sem=send, recv_sem=recv, device_id={"img": to}, device_id_type=MESH
        )

    def piece_of(r, k):
        row = pl.multiple_of(lax.rem(k, round_parts) * width, width)
        col = pl.multiple_of((r * round_chunks + k // round_parts) * LANES, LANES)
        return desc.at[0, pl.ds(row, width), pl.ds(col, LANES)]

    def attr_piece(c):
        return attr.at[0, :, pl.ds(pl.multiple_of(c * LANES, LANES), LANES)]

    def copy_want(k, source):
        return remote(want_out, want_all.at[source], want_ss.at[k], want_rs.at[source], k)

    def copy_attr_one(c, source):
        return remote(attr_piece(c), attr_in.at[source], attr_ss1.at[c], attr_rs1.at[source], c * parts)

    def copy_attr_two(k, source):
        return remote(attr_stage.at[k], attr_other.at[source], attr_ss2.at[k], attr_rs2.at[source], k)

    def copy_one(r, k, source):
        return remote(piece_of(r, k), pieces[r].at[source], ss1.at[r, k], rs1.at[r, source], k)

    def copy_two(r, k, source):
        return remote(stage.at[r, k], partner.at[r, source], ss2.at[r, k], rs2.at[r, source], k)

    def copy_stats(k, source):
        return remote(stats_out.at[k // parts], stats_in.at[source], ss3.at[k], rs3.at[source], k)

    def copy_merged(q, k, source_chunk):
        return remote(merged_out.at[q], merged_in.at[source_chunk], ss4.at[q], rs4.at[source_chunk], k)

    def copy_direct(i, k, source):
        return remote(stats_out.at[early + i], direct_in.at[i, source], ss5.at[i, k], rs5.at[i, source], k)

    barrier = pltpu.get_barrier_semaphore()

    @pl.loop(1, n)
    def _(step):
        pl.semaphore_signal(barrier, inc=1, device_id={"img": peer(step)}, device_id_type=MESH)

    local_copies = [
        pltpu.make_async_copy(pairs, pairs_s, local_sem.at[0]),
        pltpu.make_async_copy(owner, owner_s, local_sem.at[1]),
        pltpu.make_async_copy(counts, counts_s, local_sem.at[2]),
        pltpu.make_async_copy(attr, own_attr, local_sem.at[3]),
        pltpu.make_async_copy(desc.at[0], own, local_sem.at[4]),
        *[pltpu.make_async_copy(piece_of(r, me), pieces[r].at[me], local_sem.at[7 + r]) for r in range(rounds)],
    ]
    for copy in local_copies:
        copy.start()
    local_attr = pltpu.make_async_copy(attr_piece(my_chunk), attr_in.at[me], local_sem.at[6])

    @pl.when(my_part == 0)
    def _():
        local_attr.start()

    for copy in local_copies[:3]:
        copy.wait()
    want = owner_s[pairs_s[0, 1]]
    count_a = counts_s[pairs_s[0, 0]]
    count_b = counts_s[pairs_s[0, 1]]
    want_row = jnp.full((1, LANES), want, jnp.int32)
    want_out[...] = want_row
    want_all[me] = want_row
    pl.semaphore_wait(barrier, n - 1)

    @pl.loop(1, n)
    def _(step):
        copy_want(peer(step), me).start()

    @pl.loop(0, chunks)
    def _(step):
        c = lax.rem(my_chunk + step, chunks)

        @pl.when(c * parts != me)
        def _():
            copy_attr_one(c, me).start()

    for r in range(rounds):
        @pl.loop(1, n)
        def _(step):
            copy_one(r, peer(step), me).start()

    for copy in local_copies[3:]:
        copy.wait()
    rows8 = with_ones(own_attr[0].astype(jnp.float32))
    own_rows[...] = rows8.astype(jnp.bfloat16)
    row_scale[...] = jnp.broadcast_to(jnp.transpose(rows8)[:, 0:1] * (1.0 / math.sqrt(depth)), (keypoints, LANES))
    for block in range(blocks):
        rows = slice(block * ROWS, (block + 1) * ROWS)
        own_t[rows, :] = jnp.transpose(own[:, rows])
    row_top[...] = jnp.full((keypoints, LANES), far_low, jnp.float32)

    @pl.loop(1, n)
    def _(step):
        k = peer(step)
        copy_want(k, k).wait_recv()

    to_scalars = pltpu.make_async_copy(want_all, want_s, local_sem.at[5])
    to_scalars.start()
    to_scalars.wait()

    @pl.when(my_part == 0)
    def _():
        local_attr.wait()

        @pl.loop(1, n)
        def _(step):
            k = peer(step)
            copy_attr_one(my_chunk, k).wait_recv()

        @pl.loop(1, n)
        def _(step):
            k = peer(step)
            attr_stage[k] = attr_in[want_s[k, 0, 0]]
            copy_attr_two(k, my_chunk).start()

        attr_other[my_chunk] = attr_in[want]

    for r in range(rounds):
        @pl.loop(1, n)
        def _(step):
            k = peer(step)
            copy_one(r, k, k).wait_recv()

        @pl.loop(1, n)
        def _(step):
            k = peer(step)
            stage[r, k] = pieces[r][want_s[k, 0, 0]]
            copy_two(r, k, me).start()

        partner[r, me] = pieces[r][want]

    for chunk in range(chunks):
        cols = slice(chunk * LANES, (chunk + 1) * LANES)

        @pl.when(chunk * parts != me)
        def _():
            copy_attr_two(chunk * parts, chunk).wait_recv()

        other8 = with_ones(attr_other[chunk].astype(jnp.float32))
        other_rows[:, cols] = other8.astype(jnp.bfloat16)
        other_scale[chunk] = other8[0:1]

    row_ix = lax.broadcasted_iota(jnp.int32, (ROWS, LANES), 0)
    lane_ix = lax.broadcasted_iota(jnp.int32, (1, LANES), 1)
    first_row = lax.broadcasted_iota(jnp.int32, (4, LANES), 0) == 0

    def score_chunk(step):
        r = step // round_chunks
        within = lax.rem(me // round_parts + step, round_chunks)
        c = r * round_chunks + within
        for part in range(round_parts):
            k = within * round_parts + part

            @pl.when(k != me)
            def _():
                copy_two(r, k, k).wait_recv()

        block_b = partner[r, pl.ds(within * round_parts, round_parts)].reshape(depth, LANES)
        scale_b = other_scale[c]
        col_valid = c * LANES + lane_ix < count_b
        col_top = jnp.full((1, LANES), far_low, jnp.float32)
        for block in range(blocks):
            rows = slice(block * ROWS, (block + 1) * ROWS)
            raw = jnp.dot(own_t[rows, :], block_b, preferred_element_type=jnp.float32)
            score = raw * row_scale[rows, :] * scale_b
            scores[c, rows, :] = score
            row_top[rows, :] = jnp.maximum(row_top[rows, :], jnp.where(col_valid, score, far_low))
            masked = jnp.where(block * ROWS + row_ix < count_a, score, far_low)
            col_top = jnp.maximum(col_top, jnp.max(masked, axis=0, keepdims=True))
        sums = jnp.zeros((8, LANES), jnp.float32)
        for block in range(blocks):
            rows = slice(block * ROWS, (block + 1) * ROWS)
            weight = jnp.where(block * ROWS + row_ix < count_a, jnp.exp(scores[c, rows, :] - col_top), 0.0)
            sums = sums + split_dot(own_rows[:, rows], weight, ((1,), (0,)))
        stats = jnp.where(first_row, col_top, sums[0:4])
        stats_out[c] = stats
        return c, within, stats

    def merge(slot, partial):
        hit = want_all[...] == slot
        tops = partial[:, 0:1, :]
        peak = jnp.maximum(jnp.max(jnp.where(hit, tops, far_low), axis=0), 0.0)
        fade = jnp.where(hit, jnp.exp(tops - peak[None]), 0.0)
        total = jnp.sum(fade * partial, axis=0)
        partition = jnp.exp(-peak) + total[1:2]
        return jnp.where(first_row, peak + jnp.log(partition), total / partition)

    @pl.loop(0, early)
    def _(step):
        c, _, stats = score_chunk(step)
        for part in range(parts):
            k = c * parts + part

            @pl.when(k != me)
            def _():
                copy_stats(k, me).start()

            @pl.when(k == me)
            def _():
                stats_in[me] = stats

    @pl.loop(early, chunks)
    def _(step):
        _, i, stats = score_chunk(step)
        direct_in[i, me] = stats

        @pl.loop(1, n)
        def _(hop):
            copy_direct(i, peer(hop), me).start()

    @pl.when(my_chunk < early)
    def _():
        @pl.loop(1, n)
        def _(step):
            k = peer(step)
            copy_stats(k, k).wait_recv()

        @pl.loop(0, chunks)
        def _(q):
            slot = my_part * chunks + q
            merged = merge(slot, stats_in[...])
            merged_out[q] = merged

            @pl.when(slot != me)
            def _():
                copy_merged(q, slot, my_chunk).start()

            @pl.when(slot == me)
            def _():
                merged_in[my_chunk] = merged

    for block in range(blocks):
        rows = slice(block * ROWS, (block + 1) * ROWS)
        top = jnp.max(row_top[rows, :], axis=1, keepdims=True)
        sums = jnp.zeros((8, ROWS), jnp.float32)
        for chunk in range(chunks):
            cols = slice(chunk * LANES, (chunk + 1) * LANES)
            weight = jnp.where(chunk * LANES + lane_ix < count_b, jnp.exp(scores[chunk, rows, :] - top), 0.0)
            sums = sums + split_dot(other_rows[:, cols], weight, ((1,), (1,)))
        row_valid = block * ROWS + lax.broadcasted_iota(jnp.int32, (2, ROWS), 1) < count_a
        match_o[0, :, rows] = jnp.where(row_valid, sums[2:4] / sums[1:2], 0.0)

    def write(chunk, result):
        cols = slice(chunk * LANES, (chunk + 1) * LANES)
        lse_o[:, cols] = result[0:1]
        xy_o[0, :, cols] = result[2:4]

    for i in range(round_chunks):
        @pl.loop(1, n)
        def _(step):
            k = peer(step)
            copy_direct(i, k, k).wait_recv()

        write(early + i, merge(me, direct_in[i]))

    home_part = me // chunks
    for chunk in range(early):
        k = chunk * parts + home_part

        @pl.when(k != me)
        def _():
            copy_merged(chunk, k, chunk).wait_recv()

        write(chunk, merged_in[chunk])

    @pl.loop(1, n)
    def _(step):
        k = peer(step)
        copy_want(k, me).wait_send()
        for r in range(rounds):
            copy_one(r, k, me).wait_send()
            copy_two(r, k, me).wait_send()
        for i in range(round_chunks):
            copy_direct(i, k, me).wait_send()

        @pl.when(k // parts < early)
        def _():
            copy_stats(k, me).wait_send()

    @pl.when(my_chunk < early)
    def _():
        @pl.loop(0, chunks)
        def _(q):
            slot = my_part * chunks + q

            @pl.when(slot != me)
            def _():
                copy_merged(q, slot, my_chunk).wait_send()

    @pl.loop(0, chunks)
    def _(c):
        @pl.when(c * parts != me)
        def _():
            copy_attr_one(c, me).wait_send()

    @pl.when(my_part == 0)
    def _():
        @pl.loop(1, n)
        def _(step):
            copy_attr_two(peer(step), my_chunk).wait_send()


def put_out(match, lse, xy, match_o, lse_o, xy_o, sem):
    copies = [
        pltpu.make_async_copy(match, match_o, sem.at[0]),
        pltpu.make_async_copy(lse, lse_o, sem.at[1]),
        pltpu.make_async_copy(xy, xy_o, sem.at[2]),
    ]
    for copy in copies:
        copy.start()
    for copy in copies:
        copy.wait()


def solution(mesh):
    n = mesh.shape["img"]

    def shards(descriptors, attributes, counts, owner_slot, pair_list):
        _, depth, keypoints = descriptors.shape
        chunks = keypoints // LANES
        parts = n // chunks
        rounds = min(ROUNDS, depth * chunks // (n * MIN_WIDTH))
        width = depth * chunks // (n * rounds)
        vmem = pl.BlockSpec(memory_space=pltpu.VMEM)
        hbm = pl.BlockSpec(memory_space=pltpu.HBM)
        f32, bf16, i32 = jnp.float32, jnp.bfloat16, jnp.int32
        sems = pltpu.SemaphoreType.DMA
        out_shape = (
            jax.ShapeDtypeStruct((1, 2, keypoints), f32),
            jax.ShapeDtypeStruct((1, keypoints), f32),
            jax.ShapeDtypeStruct((1, 2, keypoints), f32),
        )
        results = pl.pallas_call(
            functools.partial(kernel, n, rounds),
            out_shape=out_shape,
            in_specs=[hbm] * 5,
            out_specs=(vmem, vmem, vmem),
            scratch_shapes=[
                pltpu.VMEM((depth, keypoints), bf16),
                pltpu.VMEM((keypoints, depth), bf16),
                pltpu.VMEM((1, 3, keypoints), bf16),
                pltpu.VMEM((keypoints, LANES), f32),
                pltpu.VMEM((8, keypoints), bf16),
                pltpu.VMEM((8, keypoints), bf16),
                pltpu.VMEM((chunks, 1, LANES), f32),
                pltpu.VMEM((1, LANES), i32),
                pltpu.VMEM((n, 1, LANES), i32),
                pltpu.SMEM((n, 1, LANES), i32),
                pltpu.SMEM(counts.shape, i32),
                pltpu.SMEM(owner_slot.shape, i32),
                pltpu.SMEM(pair_list.shape, i32),
                pltpu.VMEM((n, 3, LANES), bf16),
                pltpu.VMEM((n, 3, LANES), bf16),
                pltpu.VMEM((chunks, 3, LANES), bf16),
                *[pltpu.VMEM((rounds, n, width, LANES), bf16)] * 2,
                pltpu.VMEM((chunks, keypoints, LANES), f32),
                pltpu.VMEM((keypoints, LANES), f32),
                pltpu.VMEM((chunks, 4, LANES), f32),
                pltpu.VMEM((n, 4, LANES), f32),
                pltpu.VMEM((chunks, 4, LANES), f32),
                pltpu.VMEM((chunks, 4, LANES), f32),
                pltpu.VMEM((chunks // rounds, n, 4, LANES), f32),
                sems((7 + rounds,)),
                *[sems((n,))] * 2,
                sems((chunks,)),
                *[sems((n,))] * 2,
                sems((chunks,)),
                *[sems((rounds, n))] * 4,
                *[sems((n,))] * 2,
                *[sems((chunks,))] * 2,
                *[sems((chunks // rounds, n))] * 2,
                *[pltpu.VMEM((n, width, LANES), bf16)] * rounds,
            ],
            compiler_params=pltpu.CompilerParams(
                collective_id=0, has_side_effects=True
            ),
        )(descriptors, attributes, counts, owner_slot, pair_list)
        return pl.pallas_call(
            put_out,
            out_shape=out_shape,
            in_specs=[vmem] * 3,
            out_specs=(hbm, hbm, hbm),
            scratch_shapes=[sems((3,))],
        )(*results)

    placed = (
        P(("groups", "img"), None, None),
        P(("groups", "img"), None, None),
        P("groups"),
        P("groups"),
        P(("groups", "img"), None),
    )
    return jax.shard_map(
        shards,
        mesh=mesh,
        in_specs=placed,
        out_specs=(
            P(("groups", "img"), None, None),
            P(("groups", "img"), None),
            P(("groups", "img"), None, None),
        ),
        check_vma=False,
    )
```

profile of v0, /device:TPU:0, one launch (start us, length us, event | category | flops | bytes accessed | tf_op | source)
XLA Modules:
  0.0 45.0 jit_solution(3876372525322771750)
XLA Ops:
  0.6 43.0 %shard_map.76 = (f32[1,2,1024]{2,1,0:T(2,128)}, f32[1,1024]{1,0:T(1,128)}, f32[1,2,1024]{2,1,0:T(2,128)}) custom-call(bf16[1,256,1024]{2,1,0:T(8,128)(2,1)} %desc.1, bf16[1,3,1024]{2,1,0:T(4,128)(2,1)} %attr.1, s32[16]{0:T(128)} %counts.1, s32[16]{0:T(128)} %owner.1, s32[1,2]{1,0:T(1,128)} %pairs.1), custom_call_target="tpu_custom_call" | custom-call | tf_op jit(solution)/shard_map/pallas_call | solution.py:394
  43.6 1.4 %shard_map.77 = (f32[1,2,1024]{2,1,0:T(2,128)}, f32[1,1024]{1,0:T(1,128)}, f32[1,2,1024]{2,1,0:T(2,128)}) custom-call(f32[1,2,1024]{2,1,0:T(2,128)} %get-tuple-element.6.match, f32[1,1024]{1,0:T(1,128)} %get-tuple-element.7.lse, f32[1,2,1024]{2,1,0:T(2,128)} %get-tuple-element.8.xy), custom_call_target="tpu_custom_call" | custom-call | tf_op jit(solution)/shard_map/pallas_call | solution.py:439
where the time goes:
time: 45.2 us; the launch traced here: 45 us
  Pallas kernels  44.3 us (98%)
  between operations  0.64 us (1%)
    pallas_call x1, Pallas kernels, shards(): pl.pallas_call(functools.partial(kernel, n, rounds), out_shape=out_shape,...  43 us
    pallas_call x1, Pallas kernels, shards(): pl.pallas_call(put_out, out_shape=out_shape, in_specs=[vmem] * 3, out_spe...  1.35 us

commit v1 on v0

--- a/solution.py
+++ b/solution.py
@@ -13,6 +13,7 @@
 ROWS = 256
 ROUNDS = 4
 MIN_WIDTH = 16
+TILE = 16
 far_low = -1e30
 
 
@@ -373,11 +374,405 @@
         copy.wait()
 
 
+def plan(keypoints):
+    half, quarter, eighth = keypoints // 2, keypoints // 4, keypoints // 8
+    spans = ((0, half + quarter), (half + quarter, quarter))
+    subs = ((0, 0, half), (0, half, quarter), (1, 0, eighth), (1, eighth, eighth))
+    return spans, subs
+
+
+def tile_kernel(
+    n, desc, attr, counts, owner, pairs, match_o, lse_o, xy_o,
+    own, own_t, own_attr, row_scale, own_rows, other_rows, other_scale, want_out, want_all, want_s,
+    counts_s, owner_s, pairs_s, attr_all, attr_stage, attr_other,
+    scores, row_top, stats_out, stats_in, merged_out, merged_in, direct_in,
+    local_sem, want_ss, want_rs, attr_ss1, attr_rs1, attr_ss2, attr_rs2,
+    ss1, rs1, ss2, rs2, ss3, rs3, ss4, rs4, ss5, rs5, *buffers,
+):
+    depth, keypoints = desc.shape[1:]
+    spans, subs = plan(keypoints)
+    pieces = buffers[: len(spans)]
+    stage = buffers[len(spans) : len(spans) + len(subs)]
+    partner = buffers[len(spans) + len(subs) :]
+    width = depth // n
+    chunks = keypoints // LANES
+    parts = n // chunks
+    blocks = keypoints // ROWS
+    direct = sum(w for r, _, w in subs if r == 1) // LANES
+    early = chunks - direct
+    team = 4
+    me = lax.axis_index("img")
+    my_chunk = me // parts
+    my_part = lax.rem(me, parts)
+    lead = me - lax.rem(me, team)
+
+    def peer(j):
+        return lax.rem(me + n // 2 + (j // 2) * (2 * lax.rem(j, 2) - 1), n)
+
+    def remote(src, dst, send, recv, to):
+        return pltpu.make_async_remote_copy(
+            src_ref=src, dst_ref=dst, send_sem=send, recv_sem=recv, device_id={"img": to}, device_id_type=MESH
+        )
+
+    def drain(like, sem):
+        pltpu.make_async_copy(like, like, sem).wait()
+
+    def others(buffer):
+        return buffer.at[pl.ds(0, n - 1)]
+
+    def piece_of(r, k):
+        first, w = spans[r]
+        return desc.at[0, pl.ds(pl.multiple_of(k * width, width), width), pl.ds(first, w)]
+
+    def copy_want(k):
+        return remote(want_out, want_all.at[me], want_ss, want_rs, k)
+
+    def copy_attr_one(k):
+        return remote(attr.at[0], attr_all.at[me], attr_ss1, attr_rs1, k)
+
+    def copy_attr_two(j, k):
+        return remote(attr_stage.at[j], attr_other, attr_ss2.at[j], attr_rs2, k)
+
+    def copy_one(r, k):
+        return remote(piece_of(r, k), pieces[r].at[me], ss1.at[r], rs1.at[r], k)
+
+    def copy_two(u, k):
+        return remote(stage[u].at[k], partner[u].at[me], ss2.at[u], rs2.at[u], k)
+
+    def copy_stats(c, k):
+        return remote(stats_out.at[c], stats_in.at[me], ss3.at[k], rs3, k)
+
+    def copy_merged(q, k, source_chunk):
+        return remote(merged_out.at[q], merged_in.at[source_chunk], ss4.at[q], rs4.at[source_chunk], k)
+
+    def copy_direct(i, k):
+        return remote(stats_out.at[early + i], direct_in.at[i, me], ss5.at[i], rs5.at[i], k)
+
+    barrier = pltpu.get_barrier_semaphore()
+
+    @pl.loop(1, n)
+    def _(step):
+        pl.semaphore_signal(barrier, inc=1, device_id={"img": peer(step)}, device_id_type=MESH)
+
+    local_copies = [
+        pltpu.make_async_copy(pairs, pairs_s, local_sem.at[0]),
+        pltpu.make_async_copy(owner, owner_s, local_sem.at[1]),
+        pltpu.make_async_copy(counts, counts_s, local_sem.at[2]),
+        pltpu.make_async_copy(attr, own_attr, local_sem.at[3]),
+        pltpu.make_async_copy(desc.at[0], own, local_sem.at[4]),
+        pltpu.make_async_copy(attr.at[0], attr_all.at[me], local_sem.at[6]),
+        *[pltpu.make_async_copy(piece_of(r, me), pieces[r].at[me], local_sem.at[7 + r]) for r in range(len(spans))],
+    ]
+    for copy in local_copies:
+        copy.start()
+    for copy in local_copies[:3]:
+        copy.wait()
+    want = owner_s[pairs_s[0, 1]]
+    count_a = counts_s[pairs_s[0, 0]]
+    count_b = counts_s[pairs_s[0, 1]]
+    want_row = jnp.full((1, LANES), want, jnp.int32)
+    want_out[...] = want_row
+    want_all[me] = want_row
+    pl.semaphore_wait(barrier, n - 1)
+
+    @pl.loop(1, n)
+    def _(step):
+        copy_want(peer(step)).start()
+
+    @pl.loop(1, n)
+    def _(step):
+        copy_one(0, peer(step)).start()
+
+    @pl.loop(0, n // team)
+    def _(t):
+        @pl.when(t * team != me)
+        def _():
+            copy_attr_one(t * team).start()
+
+    @pl.loop(1, n)
+    def _(step):
+        copy_one(1, peer(step)).start()
+
+    for copy in local_copies[3:]:
+        copy.wait()
+    rows8 = with_ones(own_attr[0].astype(jnp.float32))
+    own_rows[...] = rows8.astype(jnp.bfloat16)
+    row_scale[...] = jnp.broadcast_to(jnp.transpose(rows8)[:, 0:1] * (1.0 / math.sqrt(depth)), (keypoints, LANES))
+    for block in range(blocks):
+        rows = slice(block * ROWS, (block + 1) * ROWS)
+        own_t[rows, :] = jnp.transpose(own[:, rows])
+    row_top[...] = jnp.full((keypoints, LANES), far_low, jnp.float32)
+
+    drain(others(want_all), want_rs)
+    to_scalars = pltpu.make_async_copy(want_all, want_s, local_sem.at[5])
+    to_scalars.start()
+    to_scalars.wait()
+
+    def forward(u):
+        r, first, w = subs[u]
+
+        @pl.loop(1, n)
+        def _(step):
+            k = peer(step)
+            stage[u][k] = pieces[r][want_s[k, 0, 0], :, first : first + w]
+            copy_two(u, k).start()
+
+        partner[u][me] = pieces[r][want, :, first : first + w]
+
+    def forward_round(r):
+        drain(others(pieces[r]), rs1.at[r])
+        for u in range(len(subs)):
+            if subs[u][0] == r:
+                forward(u)
+
+    forward_round(0)
+
+    @pl.when(me == lead)
+    def _():
+        drain(others(attr_all), attr_rs1)
+        for j in range(1, team):
+            attr_stage[j] = attr_all[want_s[me + j, 0, 0]]
+            copy_attr_two(j, me + j).start()
+        attr_other[...] = attr_all[want]
+
+    forward_round(1)
+
+    @pl.when(me != lead)
+    def _():
+        drain(attr_other, attr_rs2)
+
+    other8 = with_ones(attr_other[...].astype(jnp.float32))
+    other_rows[...] = other8.astype(jnp.bfloat16)
+    for chunk in range(chunks):
+        other_scale[chunk] = other8[0:1, chunk * LANES : (chunk + 1) * LANES]
+
+    row_ix = lax.broadcasted_iota(jnp.int32, (ROWS, LANES), 0)
+    lane_ix = lax.broadcasted_iota(jnp.int32, (1, LANES), 1)
+    first_row = lax.broadcasted_iota(jnp.int32, (4, LANES), 0) == 0
+
+    def score_chunk(u, i, c):
+        cols = pl.ds(pl.multiple_of(i * LANES, LANES), LANES)
+        block_b = partner[u][:, :, cols].reshape(depth, LANES)
+        scale_b = other_scale[c]
+        col_valid = c * LANES + lane_ix < count_b
+        col_top = jnp.full((1, LANES), far_low, jnp.float32)
+        for block in range(blocks):
+            rows = slice(block * ROWS, (block + 1) * ROWS)
+            raw = jnp.dot(own_t[rows, :], block_b, preferred_element_type=jnp.float32)
+            score = raw * row_scale[rows, :] * scale_b
+            scores[c, rows, :] = score
+            row_top[rows, :] = jnp.maximum(row_top[rows, :], jnp.where(col_valid, score, far_low))
+            masked = jnp.where(block * ROWS + row_ix < count_a, score, far_low)
+            col_top = jnp.maximum(col_top, jnp.max(masked, axis=0, keepdims=True))
+        sums = jnp.zeros((8, LANES), jnp.float32)
+        for block in range(blocks):
+            rows = slice(block * ROWS, (block + 1) * ROWS)
+            weight = jnp.where(block * ROWS + row_ix < count_a, jnp.exp(scores[c, rows, :] - col_top), 0.0)
+            sums = sums + split_dot(own_rows[:, rows], weight, ((1,), (0,)))
+        stats = jnp.where(first_row, col_top, sums[0:4])
+        stats_out[c] = stats
+        return stats
+
+    def merge(slot, partial):
+        hit = want_all[...] == slot
+        tops = partial[:, 0:1, :]
+        peak = jnp.maximum(jnp.max(jnp.where(hit, tops, far_low), axis=0), 0.0)
+        fade = jnp.where(hit, jnp.exp(tops - peak[None]), 0.0)
+        total = jnp.sum(fade * partial, axis=0)
+        partition = jnp.exp(-peak) + total[1:2]
+        return jnp.where(first_row, peak + jnp.log(partition), total / partition)
+
+    for u in range(len(subs)):
+        r, first, w = subs[u]
+        base = (spans[r][0] + first) // LANES
+        drain(others(partner[u]), rs2.at[u])
+        if r == 0:
+            @pl.loop(0, w // LANES)
+            def _(i):
+                c = base + i
+                stats = score_chunk(u, i, c)
+                for part in range(parts):
+                    k = c * parts + part
+
+                    @pl.when(k != me)
+                    def _():
+                        copy_stats(c, k).start()
+
+                    @pl.when(k == me)
+                    def _():
+                        stats_in[me] = stats
+        else:
+            for i in range(w // LANES):
+                d = base + i - early
+                direct_in[d, me] = score_chunk(u, i, base + i)
+
+                @pl.loop(1, n)
+                def _(step):
+                    copy_direct(d, peer(step)).start()
+
+    @pl.when(my_chunk < early)
+    def _():
+        drain(others(stats_in), rs3)
+
+        @pl.loop(0, chunks)
+        def _(q):
+            slot = my_part * chunks + q
+            merged = merge(slot, stats_in[...])
+            merged_out[q] = merged
+
+            @pl.when(slot != me)
+            def _():
+                copy_merged(q, slot, my_chunk).start()
+
+            @pl.when(slot == me)
+            def _():
+                merged_in[my_chunk] = merged
+
+    for block in range(blocks):
+        rows = slice(block * ROWS, (block + 1) * ROWS)
+        top = jnp.max(row_top[rows, :], axis=1, keepdims=True)
+        sums = jnp.zeros((8, ROWS), jnp.float32)
+        for chunk in range(chunks):
+            cols = slice(chunk * LANES, (chunk + 1) * LANES)
+            weight = jnp.where(chunk * LANES + lane_ix < count_b, jnp.exp(scores[chunk, rows, :] - top), 0.0)
+            sums = sums + split_dot(other_rows[:, cols], weight, ((1,), (1,)))
+        row_valid = block * ROWS + lax.broadcasted_iota(jnp.int32, (2, ROWS), 1) < count_a
+        match_o[0, :, rows] = jnp.where(row_valid, sums[2:4] / sums[1:2], 0.0)
+
+    def write(chunk, result):
+        cols = slice(chunk * LANES, (chunk + 1) * LANES)
+        lse_o[:, cols] = result[0:1]
+        xy_o[0, :, cols] = result[2:4]
+
+    drain(others(want_all), want_ss)
+    for r in range(len(spans)):
+        drain(others(pieces[r]), ss1.at[r])
+    for u in range(len(subs)):
+        drain(others(partner[u]), ss2.at[u])
+
+    @pl.loop(0, n // team)
+    def _(t):
+        @pl.when(t * team != me)
+        def _():
+            drain(attr_other, attr_ss1)
+
+    @pl.when(me == lead)
+    def _():
+        for j in range(1, team):
+            copy_attr_two(j, me + j).wait_send()
+
+    @pl.loop(0, early * parts)
+    def _(k):
+        @pl.when(k != me)
+        def _():
+            copy_stats(k // parts, k).wait_send()
+
+    for i in range(direct):
+        drain(others(direct_in.at[i]), rs5.at[i])
+        write(early + i, merge(me, direct_in[i]))
+
+    home_part = me // chunks
+    for chunk in range(early):
+        k = chunk * parts + home_part
+
+        @pl.when(k != me)
+        def _():
+            copy_merged(0, k, chunk).wait_recv()
+
+        write(chunk, merged_in[chunk])
+
+    for i in range(direct):
+        drain(others(direct_in.at[i]), ss5.at[i])
+
+    @pl.when(my_chunk < early)
+    def _():
+        @pl.loop(0, chunks)
+        def _(q):
+            slot = my_part * chunks + q
+
+            @pl.when(slot != me)
+            def _():
+                copy_merged(q, slot, my_chunk).wait_send()
+
+
+def one_tile(n, descriptors, attributes, counts, owner_slot, pair_list):
+    _, depth, keypoints = descriptors.shape
+    chunks = keypoints // LANES
+    spans, subs = plan(keypoints)
+    width = depth // n
+    direct = sum(w for r, _, w in subs if r == 1) // LANES
+    vmem = pl.BlockSpec(memory_space=pltpu.VMEM)
+    hbm = pl.BlockSpec(memory_space=pltpu.HBM)
+    f32, bf16, i32 = jnp.float32, jnp.bfloat16, jnp.int32
+    sems = pltpu.SemaphoreType.DMA
+    out_shape = (
+        jax.ShapeDtypeStruct((1, 2, keypoints), f32),
+        jax.ShapeDtypeStruct((1, keypoints), f32),
+        jax.ShapeDtypeStruct((1, 2, keypoints), f32),
+    )
+    results = pl.pallas_call(
+        functools.partial(tile_kernel, n),
+        out_shape=out_shape,
+        in_specs=[hbm] * 5,
+        out_specs=(vmem, vmem, vmem),
+        scratch_shapes=[
+            pltpu.VMEM((depth, keypoints), bf16),
+            pltpu.VMEM((keypoints, depth), bf16),
+            pltpu.VMEM((1, 3, keypoints), bf16),
+            pltpu.VMEM((keypoints, LANES), f32),
+            pltpu.VMEM((8, keypoints), bf16),
+            pltpu.VMEM((8, keypoints), bf16),
+            pltpu.VMEM((chunks, 1, LANES), f32),
+            pltpu.VMEM((1, LANES), i32),
+            pltpu.VMEM((n, 1, LANES), i32),
+            pltpu.SMEM((n, 1, LANES), i32),
+            pltpu.SMEM(counts.shape, i32),
+            pltpu.SMEM(owner_slot.shape, i32),
+            pltpu.SMEM(pair_list.shape, i32),
+            pltpu.VMEM((n, 3, keypoints), bf16),
+            pltpu.VMEM((4, 3, keypoints), bf16),
+            pltpu.VMEM((3, keypoints), bf16),
+            pltpu.VMEM((chunks, keypoints, LANES), f32),
+            pltpu.VMEM((keypoints, LANES), f32),
+            pltpu.VMEM((chunks, 4, LANES), f32),
+            pltpu.VMEM((n, 4, LANES), f32),
+            pltpu.VMEM((chunks, 4, LANES), f32),
+            pltpu.VMEM((chunks, 4, LANES), f32),
+            pltpu.VMEM((direct, n, 4, LANES), f32),
+            sems((7 + len(spans),)),
+            sems,
+            sems,
+            sems,
+            sems,
+            sems((4,)),
+            sems,
+            *[sems((len(spans),))] * 2,
+            *[sems((len(subs),))] * 2,
+            sems((n,)),
+            sems,
+            *[sems((chunks,))] * 2,
+            *[sems((direct,))] * 2,
+            *[pltpu.VMEM((n, width, w), bf16) for _, w in spans],
+            *[pltpu.VMEM((n, width, w), bf16) for _, _, w in subs] * 2,
+        ],
+        compiler_params=pltpu.CompilerParams(collective_id=0, has_side_effects=True),
+    )(descriptors, attributes, counts, owner_slot, pair_list)
+    return pl.pallas_call(
+        put_out,
+        out_shape=out_shape,
+        in_specs=[vmem] * 3,
+        out_specs=(hbm, hbm, hbm),
+        scratch_shapes=[sems((3,))],
+    )(*results)
+
+
 def solution(mesh):
     n = mesh.shape["img"]
 
     def shards(descriptors, attributes, counts, owner_slot, pair_list):
         _, depth, keypoints = descriptors.shape
+        if n * TILE == depth:
+            return one_tile(n, descriptors, attributes, counts, owner_slot, pair_list)
         chunks = keypoints // LANES
         parts = n // chunks
         rounds = min(ROUNDS, depth * chunks // (n * MIN_WIDTH))

time: 45.2 us -> 42.1 us (0.931)
  Pallas kernels: 44.3 us -> 41.3 us
    pallas_call x2, Pallas kernels: 44.3 us -> 41.3 us  [the longest x1 40 us: one_tile(): pl.pallas_call(functools.partial(tile_kernel, n), out_shape=out_shape, in...]
where the time goes in v1:
time: 42.1 us; the launch traced here: 42 us
  Pallas kernels  41.3 us (98%)
  between operations  0.64 us (2%)
    pallas_call x1, Pallas kernels, one_tile(): pl.pallas_call(functools.partial(tile_kernel, n), out_shape=out_shape, in...  40 us
    pallas_call x1, Pallas kernels, one_tile(): pl.pallas_call(put_out, out_shape=out_shape, in_specs=[vmem] * 3, out_spe...  1.35 us

profile of v1, /device:TPU:0, one launch (start us, length us, event | category | flops | bytes accessed | tf_op | source)
XLA Modules:
  0.0 42.0 jit_solution(13063050438898306387)
XLA Ops:
  0.6 40.0 %shard_map.76 = (f32[1,2,1024]{2,1,0:T(2,128)}, f32[1,1024]{1,0:T(1,128)}, f32[1,2,1024]{2,1,0:T(2,128)}) custom-call(bf16[1,256,1024]{2,1,0:T(8,128)(2,1)} %desc.1, bf16[1,3,1024]{2,1,0:T(4,128)(2,1)} %attr.1, s32[16]{0:T(128)} %counts.1, s32[16]{0:T(128)} %owner.1, s32[1,2]{1,0:T(1,128)} %pairs.1), custom_call_target="tpu_custom_call" | custom-call | tf_op jit(solution)/shard_map/pallas_call | solution.py:713
  40.6 1.4 %shard_map.77 = (f32[1,2,1024]{2,1,0:T(2,128)}, f32[1,1024]{1,0:T(1,128)}, f32[1,2,1024]{2,1,0:T(2,128)}) custom-call(f32[1,2,1024]{2,1,0:T(2,128)} %get-tuple-element.6.match, f32[1,1024]{1,0:T(1,128)} %get-tuple-element.7.lse, f32[1,2,1024]{2,1,0:T(2,128)} %get-tuple-element.8.xy), custom_call_target="tpu_custom_call" | custom-call | tf_op jit(solution)/shard_map/pallas_call | solution.py:760

commit v2 on v1

--- a/solution.py
+++ b/solution.py
@@ -406,8 +406,19 @@
     my_part = lax.rem(me, parts)
     lead = me - lax.rem(me, team)
 
-    def peer(j):
-        return lax.rem(me + n // 2 + (j // 2) * (2 * lax.rem(j, 2) - 1), n)
+    seat = lax.rem(me, team)
+    upper = (2 * me) // n
+
+    def each_peer(act):
+        @pl.loop(0, n)
+        def _(step):
+            row = step // team
+            far = upper * row + (1 - upper) * (n // team - 1 - row)
+            k = far * team + lax.rem(seat + step, team)
+
+            @pl.when(k != me)
+            def _():
+                act(k)
 
     def remote(src, dst, send, recv, to):
         return pltpu.make_async_remote_copy(
@@ -450,9 +461,7 @@
 
     barrier = pltpu.get_barrier_semaphore()
 
-    @pl.loop(1, n)
-    def _(step):
-        pl.semaphore_signal(barrier, inc=1, device_id={"img": peer(step)}, device_id_type=MESH)
+    each_peer(lambda k: pl.semaphore_signal(barrier, inc=1, device_id={"img": k}, device_id_type=MESH))
 
     local_copies = [
         pltpu.make_async_copy(pairs, pairs_s, local_sem.at[0]),
@@ -475,13 +484,8 @@
     want_all[me] = want_row
     pl.semaphore_wait(barrier, n - 1)
 
-    @pl.loop(1, n)
-    def _(step):
-        copy_want(peer(step)).start()
-
-    @pl.loop(1, n)
-    def _(step):
-        copy_one(0, peer(step)).start()
+    each_peer(lambda k: copy_want(k).start())
+    each_peer(lambda k: copy_one(0, k).start())
 
     @pl.loop(0, n // team)
     def _(t):
@@ -489,9 +493,7 @@
         def _():
             copy_attr_one(t * team).start()
 
-    @pl.loop(1, n)
-    def _(step):
-        copy_one(1, peer(step)).start()
+    each_peer(lambda k: copy_one(1, k).start())
 
     for copy in local_copies[3:]:
         copy.wait()
@@ -511,11 +513,11 @@
     def forward(u):
         r, first, w = subs[u]
 
-        @pl.loop(1, n)
-        def _(step):
-            k = peer(step)
+        def send(k):
             stage[u][k] = pieces[r][want_s[k, 0, 0], :, first : first + w]
             copy_two(u, k).start()
+
+        each_peer(send)
 
         partner[u][me] = pieces[r][want, :, first : first + w]
 
@@ -606,9 +608,7 @@
                 d = base + i - early
                 direct_in[d, me] = score_chunk(u, i, base + i)
 
-                @pl.loop(1, n)
-                def _(step):
-                    copy_direct(d, peer(step)).start()
+                each_peer(lambda k: copy_direct(d, k).start())
 
     @pl.when(my_chunk < early)
     def _():
@@ -705,14 +705,11 @@
     hbm = pl.BlockSpec(memory_space=pltpu.HBM)
     f32, bf16, i32 = jnp.float32, jnp.bfloat16, jnp.int32
     sems = pltpu.SemaphoreType.DMA
-    out_shape = (
-        jax.ShapeDtypeStruct((1, 2, keypoints), f32),
-        jax.ShapeDtypeStruct((1, keypoints), f32),
-        jax.ShapeDtypeStruct((1, 2, keypoints), f32),
-    )
+    shapes = (1, 2, keypoints), (1, keypoints), (1, 2, keypoints)
+    out_shape = tuple(jax.ShapeDtypeStruct(shape, f32) for shape in shapes)
     results = pl.pallas_call(
         functools.partial(tile_kernel, n),
-        out_shape=out_shape,
+        out_shape=tuple(pltpu.VMEM(shape, f32) for shape in shapes),
         in_specs=[hbm] * 5,
         out_specs=(vmem, vmem, vmem),
         scratch_shapes=[
@@ -763,7 +760,7 @@
         in_specs=[vmem] * 3,
         out_specs=(hbm, hbm, hbm),
         scratch_shapes=[sems((3,))],
-    )(*results)
+    )(*[pltpu.with_memory_space_constraint(result, pltpu.VMEM) for result in results])
 
 
 def solution(mesh):

time: 42.1 us -> 40.2 us (0.955)
  Pallas kernels: 41.3 us -> 39.4 us
    pallas_call x1, Pallas kernels: 40 us -> 38.8 us  [one_tile(): pl.pallas_call(functools.partial(tile_kernel, n), out_shape=tuple((pltpu....]
    pallas_call x1, Pallas kernels: 1.35 us -> 0.64 us  [one_tile(): pl.pallas_call(put_out, out_shape=out_shape, in_specs=[vmem] * 3, out_spe...]
where the time goes in v2:
time: 40.2 us; the launch traced here: 40 us
  Pallas kernels  39.4 us (98%)
  between operations  0.64 us (2%)
    pallas_call x1, Pallas kernels, one_tile(): pl.pallas_call(functools.partial(tile_kernel, n), out_shape=tuple((pltpu....  38.8 us

profile of v2, /device:TPU:0, one launch (start us, length us, event | category | flops | bytes accessed | tf_op | source)
XLA Modules:
  0.0 40.0 jit_solution(6467958773528784774)
XLA Ops:
  0.6 38.8 %shard_map.76 = (f32[1,2,1024]{2,1,0:T(2,128)S(1)}, f32[1,1024]{1,0:T(1,128)S(1)}, f32[1,2,1024]{2,1,0:T(2,128)S(1)}) custom-call(bf16[1,256,1024]{2,1,0:T(8,128)(2,1)} %desc.1, bf16[1,3,1024]{2,1,0:T(4,128)(2,1)} %attr.1, s32[16]{0:T(128)} %counts.1, s32[16]{0:T(128)} %owner.1, s32[1,2]{1,0:T(1,128)} %pairs.1), custom_call_target="tpu_custom_call" | custom-call | tf_op jit(solution)/shard_map/pallas_call | solution.py:710
  39.4 0.6 %shard_map.77 = (f32[1,2,1024]{2,1,0:T(2,128)}, f32[1,1024]{1,0:T(1,128)}, f32[1,2,1024]{2,1,0:T(2,128)}) custom-call(f32[1,2,1024]{2,1,0:T(2,128)S(1)} %get-tuple-element.6.match, f32[1,1024]{1,0:T(1,128)S(1)} %get-tuple-element.7.lse, f32[1,2,1024]{2,1,0:T(2,128)S(1)} %get-tuple-element.8.xy), custom_call_target="tpu_custom_call" | custom-call | tf_op jit(solution)/shard_map/pallas_call | solution.py:757

commit v3 on v2

--- a/solution.py
+++ b/solution.py
@@ -385,7 +385,7 @@
     n, desc, attr, counts, owner, pairs, match_o, lse_o, xy_o,
     own, own_t, own_attr, row_scale, own_rows, other_rows, other_scale, want_out, want_all, want_s,
     counts_s, owner_s, pairs_s, attr_all, attr_stage, attr_other,
-    scores, row_top, stats_out, stats_in, merged_out, merged_in, direct_in,
+    scores, stats_out, stats_in, merged_out, merged_in, direct_in,
     local_sem, want_ss, want_rs, attr_ss1, attr_rs1, attr_ss2, attr_rs2,
     ss1, rs1, ss2, rs2, ss3, rs3, ss4, rs4, ss5, rs5, *buffers,
 ):
@@ -400,25 +400,36 @@
     blocks = keypoints // ROWS
     direct = sum(w for r, _, w in subs if r == 1) // LANES
     early = chunks - direct
-    team = 4
+    team = n // 4
     me = lax.axis_index("img")
     my_chunk = me // parts
     my_part = lax.rem(me, parts)
     lead = me - lax.rem(me, team)
 
     seat = lax.rem(me, team)
-    upper = (2 * me) // n
+    my_row = me // team
+    upper = my_row // 2
+    lower = 1 - upper
+
+    def each_in(rows, first, gap, act):
+        @pl.loop(0, rows * team)
+        def _(step):
+            i = step // team
+            row = lower * (rows - 1 - i) + upper * i
+            k = (first + gap * row) * team + lax.rem(seat + step, team)
+
+            @pl.when(k != me)
+            def _():
+                act(k)
 
     def each_peer(act):
-        @pl.loop(0, n)
-        def _(step):
-            row = step // team
-            far = upper * row + (1 - upper) * (n // team - 1 - row)
-            k = far * team + lax.rem(seat + step, team)
-
-            @pl.when(k != me)
-            def _():
-                act(k)
+        each_in(4, 0, 1, act)
+
+    def each_inner(act):
+        each_in(2, 1, 1, act)
+
+    def each_outer(act):
+        each_in(2, 0, 3, act)
 
     def remote(src, dst, send, recv, to):
         return pltpu.make_async_remote_copy(
@@ -461,7 +472,14 @@
 
     barrier = pltpu.get_barrier_semaphore()
 
-    each_peer(lambda k: pl.semaphore_signal(barrier, inc=1, device_id={"img": k}, device_id_type=MESH))
+    inner = jnp.logical_or(my_row == 1, my_row == 2)
+
+    def tell(k):
+        pl.semaphore_signal(barrier, inc=1, device_id={"img": k}, device_id_type=MESH)
+
+    @pl.when(inner)
+    def _():
+        each_inner(tell)
 
     local_copies = [
         pltpu.make_async_copy(pairs, pairs_s, local_sem.at[0]),
@@ -474,6 +492,7 @@
     ]
     for copy in local_copies:
         copy.start()
+
     for copy in local_copies[:3]:
         copy.wait()
     want = owner_s[pairs_s[0, 1]]
@@ -482,10 +501,28 @@
     want_row = jnp.full((1, LANES), want, jnp.int32)
     want_out[...] = want_row
     want_all[me] = want_row
-    pl.semaphore_wait(barrier, n - 1)
-
-    each_peer(lambda k: copy_want(k).start())
-    each_peer(lambda k: copy_one(0, k).start())
+
+    @pl.when(inner)
+    def _():
+        pl.semaphore_wait(barrier, 2 * team - 1)
+        each_outer(tell)
+        each_inner(lambda k: copy_want(k).start())
+        each_inner(lambda k: copy_one(0, k).start())
+        pl.semaphore_wait(barrier, 2 * team)
+        each_outer(tell)
+        each_outer(lambda k: copy_want(k).start())
+        each_outer(lambda k: copy_one(0, k).start())
+
+    @pl.when(jnp.logical_not(inner))
+    def _():
+        pl.semaphore_wait(barrier, 2 * team)
+        each_inner(tell)
+        each_inner(lambda k: copy_want(k).start())
+        each_inner(lambda k: copy_one(0, k).start())
+        pl.semaphore_wait(barrier, 2 * team)
+        each_outer(lambda k: copy_want(k).start())
+        each_outer(lambda k: copy_one(0, k).start())
+
 
     @pl.loop(0, n // team)
     def _(t):
@@ -503,7 +540,6 @@
     for block in range(blocks):
         rows = slice(block * ROWS, (block + 1) * ROWS)
         own_t[rows, :] = jnp.transpose(own[:, rows])
-    row_top[...] = jnp.full((keypoints, LANES), far_low, jnp.float32)
 
     drain(others(want_all), want_rs)
     to_scalars = pltpu.make_async_copy(want_all, want_s, local_sem.at[5])
@@ -556,14 +592,12 @@
         cols = pl.ds(pl.multiple_of(i * LANES, LANES), LANES)
         block_b = partner[u][:, :, cols].reshape(depth, LANES)
         scale_b = other_scale[c]
-        col_valid = c * LANES + lane_ix < count_b
         col_top = jnp.full((1, LANES), far_low, jnp.float32)
         for block in range(blocks):
             rows = slice(block * ROWS, (block + 1) * ROWS)
             raw = jnp.dot(own_t[rows, :], block_b, preferred_element_type=jnp.float32)
             score = raw * row_scale[rows, :] * scale_b
             scores[c, rows, :] = score
-            row_top[rows, :] = jnp.maximum(row_top[rows, :], jnp.where(col_valid, score, far_low))
             masked = jnp.where(block * ROWS + row_ix < count_a, score, far_low)
             col_top = jnp.maximum(col_top, jnp.max(masked, axis=0, keepdims=True))
         sums = jnp.zeros((8, LANES), jnp.float32)
@@ -630,7 +664,10 @@
 
     for block in range(blocks):
         rows = slice(block * ROWS, (block + 1) * ROWS)
-        top = jnp.max(row_top[rows, :], axis=1, keepdims=True)
+        top = jnp.full((ROWS, LANES), far_low, jnp.float32)
+        for chunk in range(chunks):
+            top = jnp.maximum(top, jnp.where(chunk * LANES + lane_ix < count_b, scores[chunk, rows, :], far_low))
+        top = jnp.max(top, axis=1, keepdims=True)
         sums = jnp.zeros((8, ROWS), jnp.float32)
         for chunk in range(chunks):
             cols = slice(chunk * LANES, (chunk + 1) * LANES)
@@ -730,7 +767,6 @@
             pltpu.VMEM((4, 3, keypoints), bf16),
             pltpu.VMEM((3, keypoints), bf16),
             pltpu.VMEM((chunks, keypoints, LANES), f32),
-            pltpu.VMEM((keypoints, LANES), f32),
             pltpu.VMEM((chunks, 4, LANES), f32),
             pltpu.VMEM((n, 4, LANES), f32),
             pltpu.VMEM((chunks, 4, LANES), f32),
@@ -768,7 +804,7 @@
 
     def shards(descriptors, attributes, counts, owner_slot, pair_list):
         _, depth, keypoints = descriptors.shape
-        if n * TILE == depth:
+        if n * TILE == depth and n % 4 == 0:
             return one_tile(n, descriptors, attributes, counts, owner_slot, pair_list)
         chunks = keypoints // LANES
         parts = n // chunks

time: 40.2 us -> 38.3 us (0.953)
  Pallas kernels: 39.4 us -> 37.5 us
    pallas_call x1, Pallas kernels: 38.8 us -> 36.8 us  [one_tile(): pl.pallas_call(functools.partial(tile_kernel, n), out_shape=tuple((pltpu....]
where the time goes in v3:
time: 38.3 us; the launch traced here: 38.1 us
  Pallas kernels  37.5 us (98%)
  between operations  0.64 us (2%)
    pallas_call x1, Pallas kernels, one_tile(): pl.pallas_call(functools.partial(tile_kernel, n), out_shape=tuple((pltpu....  36.8 us

profile of v3, /device:TPU:0, one launch (start us, length us, event | category | flops | bytes accessed | tf_op | source)
XLA Modules:
  0.0 38.1 jit_solution(6089450701293767009)
XLA Ops:
  0.6 36.8 %shard_map.76 = (f32[1,2,1024]{2,1,0:T(2,128)S(1)}, f32[1,1024]{1,0:T(1,128)S(1)}, f32[1,2,1024]{2,1,0:T(2,128)S(1)}) custom-call(bf16[1,256,1024]{2,1,0:T(8,128)(2,1)} %desc.1, bf16[1,3,1024]{2,1,0:T(4,128)(2,1)} %attr.1, s32[16]{0:T(128)} %counts.1, s32[16]{0:T(128)} %owner.1, s32[1,2]{1,0:T(1,128)} %pairs.1), custom_call_target="tpu_custom_call" | custom-call | tf_op jit(solution)/shard_map/pallas_call | solution.py:747
  37.5 0.6 %shard_map.77 = (f32[1,2,1024]{2,1,0:T(2,128)}, f32[1,1024]{1,0:T(1,128)}, f32[1,2,1024]{2,1,0:T(2,128)}) custom-call(f32[1,2,1024]{2,1,0:T(2,128)S(1)} %get-tuple-element.6.match, f32[1,1024]{1,0:T(1,128)S(1)} %get-tuple-element.7.lse, f32[1,2,1024]{2,1,0:T(2,128)S(1)} %get-tuple-element.8.xy), custom_call_target="tpu_custom_call" | custom-call | tf_op jit(solution)/shard_map/pallas_call | solution.py:793

commit v4 on v3

--- a/solution.py
+++ b/solution.py
@@ -374,10 +374,13 @@
         copy.wait()
 
 
+MERGED_SUBS = 1
+
+
 def plan(keypoints):
     half, quarter, eighth = keypoints // 2, keypoints // 4, keypoints // 8
     spans = ((0, half + quarter), (half + quarter, quarter))
-    subs = ((0, 0, half), (0, half, quarter), (1, 0, eighth), (1, eighth, eighth))
+    subs = ((0, 0, half), (0, half, quarter), (1, 0, quarter))
     return spans, subs
 
 
@@ -385,7 +388,7 @@
     n, desc, attr, counts, owner, pairs, match_o, lse_o, xy_o,
     own, own_t, own_attr, row_scale, own_rows, other_rows, other_scale, want_out, want_all, want_s,
     counts_s, owner_s, pairs_s, attr_all, attr_stage, attr_other,
-    scores, stats_out, stats_in, merged_out, merged_in, direct_in,
+    scores, stats_out, stats_in, merged_out, merged_in,
     local_sem, want_ss, want_rs, attr_ss1, attr_rs1, attr_ss2, attr_rs2,
     ss1, rs1, ss2, rs2, ss3, rs3, ss4, rs4, ss5, rs5, *buffers,
 ):
@@ -393,23 +396,27 @@
     spans, subs = plan(keypoints)
     pieces = buffers[: len(spans)]
     stage = buffers[len(spans) : len(spans) + len(subs)]
-    partner = buffers[len(spans) + len(subs) :]
+    partner = buffers[len(spans) + len(subs) : len(spans) + 2 * len(subs)]
+    late = MERGED_SUBS
+    direct_out = buffers[len(spans) + 2 * len(subs) : len(spans) + 3 * len(subs) - late]
+    direct_in = buffers[len(spans) + 3 * len(subs) - late :]
     width = depth // n
     chunks = keypoints // LANES
     parts = n // chunks
     blocks = keypoints // ROWS
-    direct = sum(w for r, _, w in subs if r == 1) // LANES
-    early = chunks - direct
+    early = sum(w for _, _, w in subs[:MERGED_SUBS]) // LANES
     team = n // 4
     me = lax.axis_index("img")
-    my_chunk = me // parts
-    my_part = lax.rem(me, parts)
-    lead = me - lax.rem(me, team)
+    my_chunk = lax.rem(me, chunks)
+    my_part = me // chunks
 
     seat = lax.rem(me, team)
     my_row = me // team
     upper = my_row // 2
     lower = 1 - upper
+    half = n // 2
+    leads = half - team, half
+    lead = lower * leads[0] + upper * leads[1]
 
     def each_in(rows, first, gap, act):
         @pl.loop(0, rows * team)
@@ -425,6 +432,13 @@
     def each_peer(act):
         each_in(4, 0, 1, act)
 
+    def each_of(first, last, act):
+        @pl.loop(first, last)
+        def _(k):
+            @pl.when(k != me)
+            def _():
+                act(k)
+
     def each_inner(act):
         each_in(2, 1, 1, act)
 
@@ -468,7 +482,7 @@
         return remote(merged_out.at[q], merged_in.at[source_chunk], ss4.at[q], rs4.at[source_chunk], k)
 
     def copy_direct(i, k):
-        return remote(stats_out.at[early + i], direct_in.at[i, me], ss5.at[i], rs5.at[i], k)
+        return remote(direct_out[i], direct_in[i].at[me], ss5.at[i], rs5.at[i], k)
 
     barrier = pltpu.get_barrier_semaphore()
 
@@ -502,6 +516,12 @@
     want_out[...] = want_row
     want_all[me] = want_row
 
+    def send_attr():
+        for k in leads:
+            @pl.when(me != k)
+            def _():
+                copy_attr_one(k).start()
+
     @pl.when(inner)
     def _():
         pl.semaphore_wait(barrier, 2 * team - 1)
@@ -524,12 +544,7 @@
         each_outer(lambda k: copy_one(0, k).start())
 
 
-    @pl.loop(0, n // team)
-    def _(t):
-        @pl.when(t * team != me)
-        def _():
-            copy_attr_one(t * team).start()
-
+    send_attr()
     each_peer(lambda k: copy_one(1, k).start())
 
     for copy in local_copies[3:]:
@@ -546,32 +561,44 @@
     to_scalars.start()
     to_scalars.wait()
 
-    def forward(u):
-        r, first, w = subs[u]
-
+    def forward(r, group):
         def send(k):
-            stage[u][k] = pieces[r][want_s[k, 0, 0], :, first : first + w]
-            copy_two(u, k).start()
+            pick = want_s[k, 0, 0]
+            for u in group:
+                _, first, w = subs[u]
+                stage[u][k] = pieces[r][pick, :, first : first + w]
+                copy_two(u, k).start()
 
         each_peer(send)
-
-        partner[u][me] = pieces[r][want, :, first : first + w]
+        for u in group:
+            _, first, w = subs[u]
+            partner[u][me] = pieces[r][want, :, first : first + w]
 
     def forward_round(r):
         drain(others(pieces[r]), rs1.at[r])
-        for u in range(len(subs)):
-            if subs[u][0] == r:
-                forward(u)
+        group = [u for u in range(len(subs)) if subs[u][0] == r]
+        if r == 0:
+            for u in group:
+                forward(r, [u])
+        else:
+            forward(r, group)
 
     forward_round(0)
-
     @pl.when(me == lead)
     def _():
         drain(others(attr_all), attr_rs1)
-        for j in range(1, team):
-            attr_stage[j] = attr_all[want_s[me + j, 0, 0]]
-            copy_attr_two(j, me + j).start()
+
+        @pl.loop(0, half)
+        def _(j):
+            k = upper * half + j
+
+            @pl.when(k != me)
+            def _():
+                attr_stage[j] = attr_all[want_s[k, 0, 0]]
+                copy_attr_two(j, k).start()
+
         attr_other[...] = attr_all[want]
+
 
     forward_round(1)
 
@@ -584,30 +611,33 @@
     for chunk in range(chunks):
         other_scale[chunk] = other8[0:1, chunk * LANES : (chunk + 1) * LANES]
 
-    row_ix = lax.broadcasted_iota(jnp.int32, (ROWS, LANES), 0)
     lane_ix = lax.broadcasted_iota(jnp.int32, (1, LANES), 1)
     first_row = lax.broadcasted_iota(jnp.int32, (4, LANES), 0) == 0
 
-    def score_chunk(u, i, c):
-        cols = pl.ds(pl.multiple_of(i * LANES, LANES), LANES)
-        block_b = partner[u][:, :, cols].reshape(depth, LANES)
-        scale_b = other_scale[c]
-        col_top = jnp.full((1, LANES), far_low, jnp.float32)
-        for block in range(blocks):
-            rows = slice(block * ROWS, (block + 1) * ROWS)
+    def score(u, first_chunk):
+        w = subs[u][2]
+        tall = ROWS // 2 if w > 2 * LANES else ROWS
+        row_ix = lax.broadcasted_iota(jnp.int32, (tall, LANES), 0)
+        lanes = [slice(i * LANES, (i + 1) * LANES) for i in range(w // LANES)]
+        block_b = partner[u][...].reshape(depth, w)
+        tops = [jnp.full((8, LANES), far_low, jnp.float32) for _ in lanes]
+        for block in range(keypoints // tall):
+            rows = slice(block * tall, (block + 1) * tall)
             raw = jnp.dot(own_t[rows, :], block_b, preferred_element_type=jnp.float32)
-            score = raw * row_scale[rows, :] * scale_b
-            scores[c, rows, :] = score
-            masked = jnp.where(block * ROWS + row_ix < count_a, score, far_low)
-            col_top = jnp.maximum(col_top, jnp.max(masked, axis=0, keepdims=True))
-        sums = jnp.zeros((8, LANES), jnp.float32)
-        for block in range(blocks):
-            rows = slice(block * ROWS, (block + 1) * ROWS)
-            weight = jnp.where(block * ROWS + row_ix < count_a, jnp.exp(scores[c, rows, :] - col_top), 0.0)
-            sums = sums + split_dot(own_rows[:, rows], weight, ((1,), (0,)))
-        stats = jnp.where(first_row, col_top, sums[0:4])
-        stats_out[c] = stats
-        return stats
+            valid = block * tall + row_ix < count_a
+            for i, cols in enumerate(lanes):
+                scaled = raw[:, cols] * row_scale[rows, :] * other_scale[first_chunk + i]
+                masked = jnp.where(valid, scaled, far_low)
+                scores[first_chunk + i, rows, :] = masked
+                tops[i] = jnp.maximum(tops[i], jnp.max(masked.reshape(tall // 8, 8, LANES), axis=0))
+        tops = [jnp.max(top, axis=0, keepdims=True) for top in tops]
+        sums = [jnp.zeros((8, LANES), jnp.float32) for _ in lanes]
+        for block in range(keypoints // tall):
+            rows = slice(block * tall, (block + 1) * tall)
+            weight = [jnp.exp(scores[first_chunk + i, rows, :] - top) for i, top in enumerate(tops)]
+            part = split_dot(own_rows[:, rows], jnp.concatenate(weight, axis=1), ((1,), (0,)))
+            sums = [total + part[:, cols] for total, cols in zip(sums, lanes)]
+        return [jnp.where(first_row, top, total[0:4]) for top, total in zip(tops, sums)]
 
     def merge(slot, partial):
         hit = want_all[...] == slot
@@ -622,13 +652,12 @@
         r, first, w = subs[u]
         base = (spans[r][0] + first) // LANES
         drain(others(partner[u]), rs2.at[u])
-        if r == 0:
-            @pl.loop(0, w // LANES)
-            def _(i):
-                c = base + i
-                stats = score_chunk(u, i, c)
+        for i, stats in enumerate(score(u, base)):
+            c = base + i
+            if u < late:
+                stats_out[c] = stats
                 for part in range(parts):
-                    k = c * parts + part
+                    k = part * chunks + c
 
                     @pl.when(k != me)
                     def _():
@@ -637,12 +666,19 @@
                     @pl.when(k == me)
                     def _():
                         stats_in[me] = stats
-        else:
-            for i in range(w // LANES):
-                d = base + i - early
-                direct_in[d, me] = score_chunk(u, i, base + i)
-
-                each_peer(lambda k: copy_direct(d, k).start())
+            else:
+                cols = slice(i * LANES, (i + 1) * LANES)
+                direct_out[u - late][:, cols] = stats
+                direct_in[u - late][me, :, cols] = stats
+        if u >= late:
+            each_of(0, team, lambda k: copy_direct(u - late, k).start())
+
+    def send_rest(k):
+        for i in range(len(subs) - late):
+            copy_direct(i, k).start()
+
+    each_of(team, n, send_rest)
+
 
     @pl.when(my_chunk < early)
     def _():
@@ -687,30 +723,45 @@
     for u in range(len(subs)):
         drain(others(partner[u]), ss2.at[u])
 
-    @pl.loop(0, n // team)
-    def _(t):
-        @pl.when(t * team != me)
+    for k in leads:
+        @pl.when(me != k)
         def _():
             drain(attr_other, attr_ss1)
 
     @pl.when(me == lead)
     def _():
-        for j in range(1, team):
-            copy_attr_two(j, me + j).wait_send()
-
-    @pl.loop(0, early * parts)
-    def _(k):
-        @pl.when(k != me)
-        def _():
-            copy_stats(k // parts, k).wait_send()
-
-    for i in range(direct):
-        drain(others(direct_in.at[i]), rs5.at[i])
-        write(early + i, merge(me, direct_in[i]))
-
-    home_part = me // chunks
+        @pl.loop(0, half)
+        def _(j):
+            k = upper * half + j
+
+            @pl.when(k != me)
+            def _():
+                copy_attr_two(j, k).wait_send()
+
+    for part in range(parts):
+        @pl.loop(0, early)
+        def _(c):
+            k = part * chunks + c
+
+            @pl.when(k != me)
+            def _():
+                copy_stats(c, k).wait_send()
+
+    for i in range(len(subs) - late):
+        drain(others(direct_in[i]), ss5.at[i])
+
+    @pl.when(my_chunk < early)
+    def _():
+        @pl.loop(0, chunks)
+        def _(q):
+            slot = my_part * chunks + q
+
+            @pl.when(slot != me)
+            def _():
+                copy_merged(q, slot, my_chunk).wait_send()
+
     for chunk in range(early):
-        k = chunk * parts + home_part
+        k = my_part * chunks + chunk
 
         @pl.when(k != me)
         def _():
@@ -718,18 +769,12 @@
 
         write(chunk, merged_in[chunk])
 
-    for i in range(direct):
-        drain(others(direct_in.at[i]), ss5.at[i])
-
-    @pl.when(my_chunk < early)
-    def _():
-        @pl.loop(0, chunks)
-        def _(q):
-            slot = my_part * chunks + q
-
-            @pl.when(slot != me)
-            def _():
-                copy_merged(q, slot, my_chunk).wait_send()
+    for u in range(late, len(subs)):
+        i = u - late
+        drain(others(direct_in[i]), rs5.at[i])
+        for j in range(subs[u][2] // LANES):
+            part = direct_in[i][:, :, j * LANES : (j + 1) * LANES]
+            write((spans[subs[u][0]][0] + subs[u][1]) // LANES + j, merge(me, part))
 
 
 def one_tile(n, descriptors, attributes, counts, owner_slot, pair_list):
@@ -737,7 +782,7 @@
     chunks = keypoints // LANES
     spans, subs = plan(keypoints)
     width = depth // n
-    direct = sum(w for r, _, w in subs if r == 1) // LANES
+    late = [w for _, _, w in subs[MERGED_SUBS:]]
     vmem = pl.BlockSpec(memory_space=pltpu.VMEM)
     hbm = pl.BlockSpec(memory_space=pltpu.HBM)
     f32, bf16, i32 = jnp.float32, jnp.bfloat16, jnp.int32
@@ -764,29 +809,30 @@
             pltpu.SMEM(owner_slot.shape, i32),
             pltpu.SMEM(pair_list.shape, i32),
             pltpu.VMEM((n, 3, keypoints), bf16),
-            pltpu.VMEM((4, 3, keypoints), bf16),
+            pltpu.VMEM((n // 2, 3, keypoints), bf16),
             pltpu.VMEM((3, keypoints), bf16),
             pltpu.VMEM((chunks, keypoints, LANES), f32),
             pltpu.VMEM((chunks, 4, LANES), f32),
             pltpu.VMEM((n, 4, LANES), f32),
             pltpu.VMEM((chunks, 4, LANES), f32),
             pltpu.VMEM((chunks, 4, LANES), f32),
-            pltpu.VMEM((direct, n, 4, LANES), f32),
             sems((7 + len(spans),)),
             sems,
             sems,
             sems,
             sems,
-            sems((4,)),
+            sems((n // 2,)),
             sems,
             *[sems((len(spans),))] * 2,
             *[sems((len(subs),))] * 2,
             sems((n,)),
             sems,
             *[sems((chunks,))] * 2,
-            *[sems((direct,))] * 2,
+            *[sems((len(late),))] * 2,
             *[pltpu.VMEM((n, width, w), bf16) for _, w in spans],
             *[pltpu.VMEM((n, width, w), bf16) for _, _, w in subs] * 2,
+            *[pltpu.VMEM((4, w), f32) for w in late],
+            *[pltpu.VMEM((n, 4, w), f32) for w in late],
         ],
         compiler_params=pltpu.CompilerParams(collective_id=0, has_side_effects=True),
     )(descriptors, attributes, counts, owner_slot, pair_list)

time: 38.3 us -> 37.3 us (0.974)
  Pallas kernels: 37.5 us -> 36.5 us
    pallas_call x1, Pallas kernels: 36.8 us -> 35.9 us  [one_tile(): pl.pallas_call(functools.partial(tile_kernel, n), out_shape=tuple((pltpu....]
where the time goes in v4:
time: 37.3 us; the launch traced here: 37.1 us
  Pallas kernels  36.5 us (98%)
  between operations  0.64 us (2%)
    pallas_call x1, Pallas kernels, one_tile(): pl.pallas_call(functools.partial(tile_kernel, n), out_shape=tuple((pltpu....  35.9 us

profile of v4, /device:TPU:0, one launch (start us, length us, event | category | flops | bytes accessed | tf_op | source)
XLA Modules:
  0.0 37.1 jit_solution(1073497194764973259)
XLA Ops:
  0.6 35.9 %shard_map.76 = (f32[1,2,1024]{2,1,0:T(2,128)S(1)}, f32[1,1024]{1,0:T(1,128)S(1)}, f32[1,2,1024]{2,1,0:T(2,128)S(1)}) custom-call(bf16[1,256,1024]{2,1,0:T(8,128)(2,1)} %desc.1, bf16[1,3,1024]{2,1,0:T(4,128)(2,1)} %attr.1, s32[16]{0:T(128)} %counts.1, s32[16]{0:T(128)} %owner.1, s32[1,2]{1,0:T(1,128)} %pairs.1), custom_call_target="tpu_custom_call" | custom-call | tf_op jit(solution)/shard_map/pallas_call | solution.py:792
  36.5 0.6 %shard_map.77 = (f32[1,2,1024]{2,1,0:T(2,128)}, f32[1,1024]{1,0:T(1,128)}, f32[1,2,1024]{2,1,0:T(2,128)}) custom-call(f32[1,2,1024]{2,1,0:T(2,128)S(1)} %get-tuple-element.6.match, f32[1,1024]{1,0:T(1,128)S(1)} %get-tuple-element.7.lse, f32[1,2,1024]{2,1,0:T(2,128)S(1)} %get-tuple-element.8.xy), custom_call_target="tpu_custom_call" | custom-call | tf_op jit(solution)/shard_map/pallas_call | solution.py:839

commit v5 on v4

--- a/solution.py
+++ b/solution.py
@@ -374,13 +374,14 @@
         copy.wait()
 
 
+SPLIT = 6
 MERGED_SUBS = 1
 
 
 def plan(keypoints):
-    half, quarter, eighth = keypoints // 2, keypoints // 4, keypoints // 8
-    spans = ((0, half + quarter), (half + quarter, quarter))
-    subs = ((0, 0, half), (0, half, quarter), (1, 0, quarter))
+    eighth = keypoints // 8
+    spans = ((0, SPLIT * eighth), (SPLIT * eighth, (8 - SPLIT) * eighth))
+    subs = ((0, 4 * eighth), (4 * eighth, 2 * eighth), (6 * eighth, 2 * eighth))
     return spans, subs
 
 
@@ -404,7 +405,7 @@
     chunks = keypoints // LANES
     parts = n // chunks
     blocks = keypoints // ROWS
-    early = sum(w for _, _, w in subs[:MERGED_SUBS]) // LANES
+    early = sum(w for _, w in subs[:MERGED_SUBS]) // LANES
     team = n // 4
     me = lax.axis_index("img")
     my_chunk = lax.rem(me, chunks)
@@ -561,29 +562,35 @@
     to_scalars.start()
     to_scalars.wait()
 
-    def forward(r, group):
+    def pick(u, index, put):
+        start, w = subs[u]
+        for r, (first, span) in enumerate(spans):
+            low, high = max(start, first), min(start + w, first + span)
+            if low < high:
+                put(slice(low - start, high - start), pieces[r][index, :, low - first : high - first])
+
+    def forward(u):
         def send(k):
-            pick = want_s[k, 0, 0]
-            for u in group:
-                _, first, w = subs[u]
-                stage[u][k] = pieces[r][pick, :, first : first + w]
-                copy_two(u, k).start()
+            def put(cols, value):
+                stage[u][k, :, cols] = value
+
+            pick(u, want_s[k, 0, 0], put)
+            copy_two(u, k).start()
 
         each_peer(send)
-        for u in group:
-            _, first, w = subs[u]
-            partner[u][me] = pieces[r][want, :, first : first + w]
-
-    def forward_round(r):
-        drain(others(pieces[r]), rs1.at[r])
-        group = [u for u in range(len(subs)) if subs[u][0] == r]
-        if r == 0:
-            for u in group:
-                forward(r, [u])
-        else:
-            forward(r, group)
-
-    forward_round(0)
+
+        def keep(cols, value):
+            partner[u][me, :, cols] = value
+
+        pick(u, want, keep)
+
+    drain(others(pieces[0]), rs1.at[0])
+    forward(0)
+
+    @pl.when(jnp.logical_not(inner))
+    def _():
+        forward(1)
+
     @pl.when(me == lead)
     def _():
         drain(others(attr_all), attr_rs1)
@@ -600,7 +607,13 @@
         attr_other[...] = attr_all[want]
 
 
-    forward_round(1)
+    drain(others(pieces[1]), rs1.at[1])
+
+    @pl.when(inner)
+    def _():
+        forward(1)
+
+    forward(2)
 
     @pl.when(me != lead)
     def _():
@@ -615,24 +628,41 @@
     first_row = lax.broadcasted_iota(jnp.int32, (4, LANES), 0) == 0
 
     def score(u, first_chunk):
-        w = subs[u][2]
-        tall = ROWS // 2 if w > 2 * LANES else ROWS
+        w = subs[u][1]
+        narrow = w == 2 * LANES
+        tall = ROWS if w == LANES else ROWS // 2
+        spot = range(keypoints // tall)
         row_ix = lax.broadcasted_iota(jnp.int32, (tall, LANES), 0)
         lanes = [slice(i * LANES, (i + 1) * LANES) for i in range(w // LANES)]
         block_b = partner[u][...].reshape(depth, w)
-        tops = [jnp.full((8, LANES), far_low, jnp.float32) for _ in lanes]
-        for block in range(keypoints // tall):
+        block_tops, block_sums = [], []
+        for block in spot:
             rows = slice(block * tall, (block + 1) * tall)
             raw = jnp.dot(own_t[rows, :], block_b, preferred_element_type=jnp.float32)
             valid = block * tall + row_ix < count_a
+            tops, weight = [], []
             for i, cols in enumerate(lanes):
                 scaled = raw[:, cols] * row_scale[rows, :] * other_scale[first_chunk + i]
                 masked = jnp.where(valid, scaled, far_low)
                 scores[first_chunk + i, rows, :] = masked
-                tops[i] = jnp.maximum(tops[i], jnp.max(masked.reshape(tall // 8, 8, LANES), axis=0))
+                if narrow:
+                    tops.append(jnp.max(masked, axis=0, keepdims=True))
+                    weight.append(jnp.exp(masked - tops[i]))
+                else:
+                    tops.append(jnp.max(masked.reshape(tall // 8, 8, LANES), axis=0))
+            block_tops.append(tops)
+            if narrow:
+                block_sums.append(split_dot(own_rows[:, rows], jnp.concatenate(weight, axis=1), ((1,), (0,))))
+        tops = [functools.reduce(jnp.maximum, [found[i] for found in block_tops]) for i in range(len(lanes))]
+        if narrow:
+            sums = [
+                sum(block_sums[block][:, cols] * jnp.exp(block_tops[block][i] - tops[i]) for block in spot)
+                for i, cols in enumerate(lanes)
+            ]
+            return [jnp.where(first_row, top, total[0:4]) for top, total in zip(tops, sums)]
         tops = [jnp.max(top, axis=0, keepdims=True) for top in tops]
         sums = [jnp.zeros((8, LANES), jnp.float32) for _ in lanes]
-        for block in range(keypoints // tall):
+        for block in spot:
             rows = slice(block * tall, (block + 1) * tall)
             weight = [jnp.exp(scores[first_chunk + i, rows, :] - top) for i, top in enumerate(tops)]
             part = split_dot(own_rows[:, rows], jnp.concatenate(weight, axis=1), ((1,), (0,)))
@@ -649,8 +679,7 @@
         return jnp.where(first_row, peak + jnp.log(partition), total / partition)
 
     for u in range(len(subs)):
-        r, first, w = subs[u]
-        base = (spans[r][0] + first) // LANES
+        base = subs[u][0] // LANES
         drain(others(partner[u]), rs2.at[u])
         for i, stats in enumerate(score(u, base)):
             c = base + i
@@ -680,25 +709,7 @@
     each_of(team, n, send_rest)
 
 
-    @pl.when(my_chunk < early)
-    def _():
-        drain(others(stats_in), rs3)
-
-        @pl.loop(0, chunks)
-        def _(q):
-            slot = my_part * chunks + q
-            merged = merge(slot, stats_in[...])
-            merged_out[q] = merged
-
-            @pl.when(slot != me)
-            def _():
-                copy_merged(q, slot, my_chunk).start()
-
-            @pl.when(slot == me)
-            def _():
-                merged_in[my_chunk] = merged
-
-    for block in range(blocks):
+    def row_block(block):
         rows = slice(block * ROWS, (block + 1) * ROWS)
         top = jnp.full((ROWS, LANES), far_low, jnp.float32)
         for chunk in range(chunks):
@@ -712,6 +723,30 @@
         row_valid = block * ROWS + lax.broadcasted_iota(jnp.int32, (2, ROWS), 1) < count_a
         match_o[0, :, rows] = jnp.where(row_valid, sums[2:4] / sums[1:2], 0.0)
 
+    row_block(0)
+    row_block(1)
+
+    @pl.when(my_chunk < early)
+    def _():
+        drain(others(stats_in), rs3)
+
+        @pl.loop(0, chunks)
+        def _(q):
+            slot = my_part * chunks + q
+            merged = merge(slot, stats_in[...])
+            merged_out[q] = merged
+
+            @pl.when(slot != me)
+            def _():
+                copy_merged(q, slot, my_chunk).start()
+
+            @pl.when(slot == me)
+            def _():
+                merged_in[my_chunk] = merged
+
+    for block in range(2, blocks):
+        row_block(block)
+
     def write(chunk, result):
         cols = slice(chunk * LANES, (chunk + 1) * LANES)
         lse_o[:, cols] = result[0:1]
@@ -772,9 +807,9 @@
     for u in range(late, len(subs)):
         i = u - late
         drain(others(direct_in[i]), rs5.at[i])
-        for j in range(subs[u][2] // LANES):
+        for j in range(subs[u][1] // LANES):
             part = direct_in[i][:, :, j * LANES : (j + 1) * LANES]
-            write((spans[subs[u][0]][0] + subs[u][1]) // LANES + j, merge(me, part))
+            write(subs[u][0] // LANES + j, merge(me, part))
 
 
 def one_tile(n, descriptors, attributes, counts, owner_slot, pair_list):
@@ -782,7 +817,7 @@
     chunks = keypoints // LANES
     spans, subs = plan(keypoints)
     width = depth // n
-    late = [w for _, _, w in subs[MERGED_SUBS:]]
+    late = [w for _, w in subs[MERGED_SUBS:]]
     vmem = pl.BlockSpec(memory_space=pltpu.VMEM)
     hbm = pl.BlockSpec(memory_space=pltpu.HBM)
     f32, bf16, i32 = jnp.float32, jnp.bfloat16, jnp.int32
@@ -830,7 +865,7 @@
             *[sems((chunks,))] * 2,
             *[sems((len(late),))] * 2,
             *[pltpu.VMEM((n, width, w), bf16) for _, w in spans],
-            *[pltpu.VMEM((n, width, w), bf16) for _, _, w in subs] * 2,
+            *[pltpu.VMEM((n, width, w), bf16) for _, w in subs] * 2,
             *[pltpu.VMEM((4, w), f32) for w in late],
             *[pltpu.VMEM((n, 4, w), f32) for w in late],
         ],

time: 37.3 us -> 37.2 us (level)
  no operation moved by 1% of the time
where the time goes in v5:
time: 37.2 us; the launch traced here: 37 us
  Pallas kernels  36.4 us (98%)
  between operations  0.64 us (2%)
    pallas_call x1, Pallas kernels, one_tile(): pl.pallas_call(functools.partial(tile_kernel, n), out_shape=tuple((pltpu....  35.7 us

profile of v5, /device:TPU:0, one launch (start us, length us, event | category | flops | bytes accessed | tf_op | source)
XLA Modules:
  0.0 37.0 jit_solution(353144027112972236)
XLA Ops:
  0.6 35.7 %shard_map.76 = (f32[1,2,1024]{2,1,0:T(2,128)S(1)}, f32[1,1024]{1,0:T(1,128)S(1)}, f32[1,2,1024]{2,1,0:T(2,128)S(1)}) custom-call(bf16[1,256,1024]{2,1,0:T(8,128)(2,1)} %desc.1, bf16[1,3,1024]{2,1,0:T(4,128)(2,1)} %attr.1, s32[16]{0:T(128)} %counts.1, s32[16]{0:T(128)} %owner.1, s32[1,2]{1,0:T(1,128)} %pairs.1), custom_call_target="tpu_custom_call" | custom-call | tf_op jit(solution)/shard_map/pallas_call | solution.py:827
  36.4 0.6 %shard_map.77 = (f32[1,2,1024]{2,1,0:T(2,128)}, f32[1,1024]{1,0:T(1,128)}, f32[1,2,1024]{2,1,0:T(2,128)}) custom-call(f32[1,2,1024]{2,1,0:T(2,128)S(1)} %get-tuple-element.6.match, f32[1,1024]{1,0:T(1,128)S(1)} %get-tuple-element.7.lse, f32[1,2,1024]{2,1,0:T(2,128)S(1)} %get-tuple-element.8.xy), custom_call_target="tpu_custom_call" | custom-call | tf_op jit(solution)/shard_map/pallas_call | solution.py:874

commit v6 on v5

--- a/solution.py
+++ b/solution.py
@@ -587,10 +587,6 @@
     drain(others(pieces[0]), rs1.at[0])
     forward(0)
 
-    @pl.when(jnp.logical_not(inner))
-    def _():
-        forward(1)
-
     @pl.when(me == lead)
     def _():
         drain(others(attr_all), attr_rs1)
@@ -609,10 +605,7 @@
 
     drain(others(pieces[1]), rs1.at[1])
 
-    @pl.when(inner)
-    def _():
-        forward(1)
-
+    forward(1)
     forward(2)
 
     @pl.when(me != lead)

time: 37.2 us -> 37.2 us (level)
  no operation moved by 1% of the time
where the time goes in v6:
time: 37.2 us; the launch traced here: 37 us
  Pallas kernels  36.4 us (98%)
  between operations  0.64 us (2%)
    pallas_call x1, Pallas kernels, one_tile(): pl.pallas_call(functools.partial(tile_kernel, n), out_shape=tuple((pltpu....  35.7 us

profile of v6, /device:TPU:0, one launch (start us, length us, event | category | flops | bytes accessed | tf_op | source)
XLA Modules:
  0.0 37.0 jit_solution(10649474818564353055)
XLA Ops:
  0.6 35.7 %shard_map.76 = (f32[1,2,1024]{2,1,0:T(2,128)S(1)}, f32[1,1024]{1,0:T(1,128)S(1)}, f32[1,2,1024]{2,1,0:T(2,128)S(1)}) custom-call(bf16[1,256,1024]{2,1,0:T(8,128)(2,1)} %desc.1, bf16[1,3,1024]{2,1,0:T(4,128)(2,1)} %attr.1, s32[16]{0:T(128)} %counts.1, s32[16]{0:T(128)} %owner.1, s32[1,2]{1,0:T(1,128)} %pairs.1), custom_call_target="tpu_custom_call" | custom-call | tf_op jit(solution)/shard_map/pallas_call | solution.py:820
  36.4 0.6 %shard_map.77 = (f32[1,2,1024]{2,1,0:T(2,128)}, f32[1,1024]{1,0:T(1,128)}, f32[1,2,1024]{2,1,0:T(2,128)}) custom-call(f32[1,2,1024]{2,1,0:T(2,128)S(1)} %get-tuple-element.6.match, f32[1,1024]{1,0:T(1,128)S(1)} %get-tuple-element.7.lse, f32[1,2,1024]{2,1,0:T(2,128)S(1)} %get-tuple-element.8.xy), custom_call_target="tpu_custom_call" | custom-call | tf_op jit(solution)/shard_map/pallas_call | solution.py:867
